TPU v7x, 512 devices: a whole 4x8x8 slice. The times are simulated.
512 devices in a mesh: tm: 8 (over z_hi, core), height: 8 (over x, z_lo), head: 8 (over y).
Axes of the slice: x: 4, y: 8, z: 8 (z_hi: 4, z_lo: 2; z = z_hi * 2 + z_lo), core: 2. Of those that a mesh axis runs over, the one named last changes fastest.
Arguments:
- lat_q: bfloat16 [8, 8, 2, 384, 3072], P('tm', 'height', None, None, 'head'), may hold values from -12 to 12
- lat_kv: bfloat16 [2, 8, 8, 2, 384, 3072], P(None, 'tm', 'height', None, None, 'head'), may hold values from -6 to 6
- txt_qkv: bfloat16 [3, 64, 128, 3072], P(None, ('tm', 'height'), None, 'head'), may hold values from -12 to 12
- blocks: int32 [8, 8, 2, 9], P('tm', 'height'), may hold values from -1 to 127, as said below
- owner: int32 [8], P('head'), may hold values from 0 to 63
Outputs:
- latent_out: bfloat16 [8, 8, 2, 384, 3072], P('tm', 'height', None, None, 'head')
- text_out: bfloat16 [128, 3072], P(None, 'head')
Inputs may be any that keep to these rules, and one draw needn't show every extreme that they name: `blocks`: row i lists its own tile i first, then distinct tiles with the same width index whose frame and height tile indices each differ from tile i's by at most one, then -1 entries; some row lists 9 tiles.
All inputs are finite; a program needn't handle non-finite values.
Results may differ from a plain program's by a relative error of at most 0.0031.
Values may be sent and summed in bfloat16 or wider, within the bound.
No kernel may reach another device: no remote copies, remote signals or barrier semaphores. Data moves between devices by JAX's collectives and lax.ppermute only.
A program may use at most 128 MiB of HBM per device.

v0:
```python
import jax
import jax.numpy as jnp
from jax import lax
from jax.sharding import PartitionSpec as P

HD = 128


def broadcast(value, axis, source):
    kept = jnp.where(lax.axis_index(axis) == source, value, 0).astype(value.dtype)
    return lax.psum(kept, axis)


def padded(x, sides, width):
    for axis, dim in sides:
        count, length = (lax.axis_size(axis), x.shape[dim])
        up = [(i, (i + 1) % count) for i in range(count - 1)]
        down = [(j, i) for i, j in up]
        last = lax.slice_in_dim(x, length - width, length, axis=dim)
        initial = lax.slice_in_dim(x, 0, width, axis=dim)
        before = lax.ppermute(last, axis, up)
        after = lax.ppermute(initial, axis, down)
        x = jnp.concatenate([before, x, after], axis=dim)
    return x


def combined_all(part, axis, combine):
    gathered = jax.tree.map(lambda a: lax.all_gather(a, axis), part)

    def take(source):
        return jax.tree.map(lambda a: lax.dynamic_index_in_dim(a, source, 0, False), gathered)

    return lax.fori_loop(
        1, lax.axis_size(axis), lambda source, state: combine(state, take(source)), take(0)
    )


def combine(first, second):
    max_first, sum_first, acc_first = first
    max_second, sum_second, acc_second = second
    merged_max = jnp.maximum(max_first, max_second)
    factor_first = jnp.exp(max_first - merged_max)
    factor_second = jnp.exp(max_second - merged_max)
    merged_sum = sum_first * factor_first + sum_second * factor_second
    merged_acc = acc_first * factor_first[..., None] + acc_second * factor_second[..., None]
    return (merged_max, merged_sum, merged_acc)


def text_part(head, text_query, key_block, value_block, inv_root):
    head_query = lax.dynamic_slice_in_dim(text_query, head * HD, HD, 1)
    head_key = lax.dynamic_slice_in_dim(key_block, head * HD, HD, 1)
    head_value = lax.dynamic_slice_in_dim(value_block, head * HD, HD, 1)
    scores = (
        jnp.einsum("qd,kd->qk", head_query, head_key, preferred_element_type=jnp.float32) * inv_root
    )
    row_max = jnp.max(scores, axis=1)
    weights = jnp.exp(scores - row_max[:, None])
    weighted = jnp.dot(weights, head_value, precision=lax.Precision.HIGHEST)
    return (row_max, jnp.sum(weights, axis=1), weighted)


def body(lat_q, lat_kv, txt_qkv, blocks, owner):
    column_count = lat_q.shape[-1]
    head_count = column_count // HD
    width_tiles = lat_q.shape[2]
    tile_rows = lat_q.shape[3]
    list_length = blocks.shape[-1]
    text_count = txt_qkv.shape[2]
    inv_root = HD ** (-0.5)
    owner_text = broadcast(txt_qkv, ("tm", "height"), owner[0])
    text_query = owner_text[0, 0]
    text_key = owner_text[1, 0]
    text_value = owner_text[2, 0]
    extended = padded(lat_kv, (("tm", 1), ("height", 2)), 1)
    near_keys = extended[0].reshape(9 * width_tiles, tile_rows, column_count)
    near_values = extended[1].reshape(9 * width_tiles, tile_rows, column_count)
    my_time = lax.axis_index("tm")
    my_height = lax.axis_index("height")
    height_count = lax.axis_size("height")
    tile_outputs = []
    for width_index in range(width_tiles):
        tile_ids = blocks[0, 0, width_index]
        listed = tile_ids >= 0
        clamped = jnp.maximum(tile_ids, 0)
        key_time = clamped // (height_count * width_tiles)
        key_height = clamped // width_tiles % height_count
        key_width = clamped % width_tiles
        position = (
            (key_time - my_time + 1) * 3 + (key_height - my_height + 1)
        ) * width_tiles + key_width
        position = jnp.where(listed, position, 0)
        key_rows = jnp.concatenate(
            [near_keys[position].reshape(list_length * tile_rows, column_count), text_key], 0
        )
        value_rows = jnp.concatenate(
            [near_values[position].reshape(list_length * tile_rows, column_count), text_value], 0
        )
        key_bias = jnp.concatenate(
            [
                jnp.repeat(jnp.where(listed, 0.0, -1e30).astype(jnp.float32), tile_rows),
                jnp.zeros((text_count,), jnp.float32),
            ]
        )
        queries = lat_q[0, 0, width_index]

        def one_head(head):
            head_query = lax.dynamic_slice_in_dim(queries, head * HD, HD, 1)
            head_key = lax.dynamic_slice_in_dim(key_rows, head * HD, HD, 1)
            head_value = lax.dynamic_slice_in_dim(value_rows, head * HD, HD, 1)
            scores = (
                jnp.einsum("qd,kd->qk", head_query, head_key, preferred_element_type=jnp.float32)
                * inv_root
                + key_bias[None, :]
            )
            row_max = jnp.max(scores, axis=1, keepdims=True)
            weights = jnp.exp(scores - row_max)
            row_sum = jnp.sum(weights, axis=1, keepdims=True)
            mixed = (
                jnp.dot(
                    weights.astype(jnp.bfloat16), head_value, preferred_element_type=jnp.float32
                )
                / row_sum
            )
            return mixed.astype(jnp.bfloat16)

        per_head = lax.map(one_head, jnp.arange(head_count, dtype=jnp.int32))
        tile_outputs.append(jnp.transpose(per_head, (1, 0, 2)).reshape(tile_rows, column_count))
    latent_out = jnp.stack(tile_outputs)[None, None]
    own_keys = lat_kv[0, 0, 0].reshape(width_tiles * tile_rows, column_count)
    own_values = lat_kv[1, 0, 0].reshape(width_tiles * tile_rows, column_count).astype(jnp.float32)

    def partial_head(head):
        return text_part(head, text_query, own_keys, own_values, inv_root)

    part_max, part_sum, part_acc = lax.map(partial_head, jnp.arange(head_count, dtype=jnp.int32))
    part_max, part_sum, part_acc = combined_all(
        (part_max, part_sum, part_acc), ("tm", "height"), combine
    )
    text_value_wide = text_value.astype(jnp.float32)

    def text_head(head):
        return text_part(head, text_query, text_key, text_value_wide, inv_root)

    own_text = lax.map(text_head, jnp.arange(head_count, dtype=jnp.int32))
    final_max, final_sum, final_acc = combine((part_max, part_sum, part_acc), own_text)
    text_mixed = final_acc / final_sum[..., None]
    text_out = (
        jnp.transpose(text_mixed, (1, 0, 2)).reshape(text_count, column_count).astype(jnp.bfloat16)
    )
    return (latent_out, text_out)


def solution(mesh):
    placed = (
        P("tm", "height", None, None, "head"),
        P(None, "tm", "height", None, None, "head"),
        P(None, ("tm", "height"), None, "head"),
        P("tm", "height", None, None),
        P("head"),
    )
    return jax.shard_map(
        body,
        mesh=mesh,
        in_specs=placed,
        out_specs=(P("tm", "height", None, None, "head"), P(None, "head")),
        check_vma=False,
    )
```

profile of v0, /device:TPU:256, one launch (start us, length us, event | category | flops | bytes accessed | tf_op | source)
XLA Modules:
  0.0 952.4 jit_solution(2615295721121671516)
XLA Ops:
  8.7 1.4 fusion.88
  10.2 190.5 %all-reduce.4.cloned.1.call-done = bf16[3,1,128,384]{3,2,1,0:T(8,128)(2,1)} async-done(((bf16[3,1,128,384]{3,2,1,0:T(8,128)(2,1)}), bf16[3,1,128,384]{3,2,1,0:T(8,128)(2,1)}) %all-reduce.4.cloned.1.call-update) | async-done | bytes 294928 | tf_op jit(solution)/shard_map/psum | solution.py:11
  200.7 1.7 fusion.79
  202.5 9.2 while.69
  211.7 1.9 collective-permute-start
  213.6 5.8 collective-permute-start.1
  219.4 21.7 %collective-permute-done = bf16[2,1,1,2,384,384]{5,4,3,2,1,0:T(8,128)(2,1)S(1)} collective-permute-done((bf16[2,1,1,2,384,384]{5,4,3,2,1,0:T(8,128)(2,1)}, bf16[2,1,1,2,384,384]{5,4,3,2,1,0:T(8,128)(2,1)S(1)}, u32[]{:S(2)}, u32[]{:S(2)}) %collective-permute-start) | collective-permute-done | bytes 1179680 | tf_op jit(solution)/shard_map/ppermute | solution.py:21
  241.3 1.5 constant_dynamic-update-slice_fusion.3
  242.8 10.3 %collective-permute-done.1 = bf16[2,1,1,2,384,384]{5,4,3,2,1,0:T(8,128)(2,1)S(1)} collective-permute-done((bf16[2,1,1,2,384,384]{5,4,3,2,1,0:T(8,128)(2,1)}, bf16[2,1,1,2,384,384]{5,4,3,2,1,0:T(8,128)(2,1)S(1)}, u32[]{:S(2)}, u32[]{:S(2)}) %collective-permute-start.1) | collective-permute-done | bytes 1179680 | tf_op jit(solution)/shard_map/ppermute | solution.py:22
  253.4 3.1 collective-permute-start.2
  256.4 1.3 collective-permute-start.3
  259.7 1.3 broadcast_in_dim.78
  260.9 1.3 reshape.383
  265.6 1.9 slice_bitcast_fusion.1
  267.5 279.3 %all-gather.4 = f32[64,3,128]{2,1,0:T(4,128)S(1)} all-gather(f32[1,3,128]{2,1,0:T(4,128)} %bitcast.216), channel_id=3, replica_groups=mesh['tm'=8,'height'=8,'head'=8] {'tm','height'}, dimensions={0}, use_global_device_ids=true | all-gather | bytes 99840 | tf_op jit(solution)/shard_map/all_gather | solution.py:28
  546.8 124.9 %all-gather.3 = f32[64,3,128]{2,1,0:T(4,128)S(1)} all-gather(f32[1,3,128]{2,1,0:T(4,128)} %bitcast.215), channel_id=2, replica_groups=mesh['tm'=8,'height'=8,'head'=8] {'tm','height'}, dimensions={0}, use_global_device_ids=true | all-gather | bytes 99840 | tf_op jit(solution)/shard_map/all_gather | solution.py:28
  674.6 23.0 %while.71 = (s32[]{:T(128)}, f32[3,128]{1,0:T(4,128)}, f32[3,128]{1,0:T(4,128)}, f32[3,128,128]{1,2,0:T(8,128)}, s32[3]{0:T(128)}, /*index=5*/bf16[128,384]{1,0:...) while((s32[]{:T(128)}, f32[3,128]{1,0:T(4,128)}, ...), condition=%wide.region_18.19_spmd, body=%wide.region_15.18_spmd.sunk | while | flops 29441796 | bytes 401111 | solution.py:144
  677.4 1.8 fusion.128
  685.1 1.8 fusion.128
  692.8 1.8 fusion.128
  697.6 8.3 pad_maximum_fusion
  705.9 9.8 %fusion.87 = (bf16[1,3,3,2,384,384]{5,4,3,2,1,0:T(8,128)(2,1)}, bf16[1,3,3,2,384,384]{5,4,3,2,1,0:T(8,128)(2,1)}) fusion(bf16[2,3,3,2,384,384]{5,4,3,2,1,0:T(8,128)(2,1)} %pad_maximum_fusion), kind=kLoop, calls=%fused_computation.133 | loop fusion | bytes 21233664 | tf_op jit(solution)/shard_map/slice | solution.py:76
  715.6 5.4 gather_fusion.1
  721.0 5.3 gather_fusion.3
  726.3 5.4 gather_fusion.2
  731.7 5.3 gather_fusion
  737.1 10.2 %pad_maximum_fusion.2 = (bf16[3584,384]{1,0:T(8,128)(2,1)}, bf16[3584,384]{1,0:T(8,128)(2,1)S(1)}, bf16[3584,384]{1,0:T(8,128)(2,1)}, bf16[3584,384]{1,0:T(8,128)(2,1)}) fusion(bf16[128,384]{1,0:T(8,128)(2,1)S(1)} %copy-done.2, bf16[3456,384]{1,0:T(8,128)(2,1)} %bitcast.205, bf16[3456,384]{1,0:T(8,128)(2,1)} %bitcast.204, bf16[128,384]{1,0:T(8,128)(2,1)S(1)} %copy-done.3, ...), kind=kLoop, calls=%fused_computation.68 | loop fusion | flops 19267584 | bytes 21823488 | tf_op jit(solution)/shard_map/concatenate | solution.py:92
  747.3 20.0 %while.67 = (s32[]{:T(128)}, bf16[3,384,128]{1,2,0:T(8,128)(2,1)S(1)}, s32[3]{0:T(128)S(1)}, bf16[384,384]{1,0:T(8,128)(2,1)}, bf16[3584,384]{1,0:T(8,128)(2,1)}...) while((s32[]{:T(128)}, ...), condition=%wide.region_4.5_spmd, body=%wide.region_1.4_spmd.sunk | while | flops 714374400 | bytes 18963120 | solution.py:126
  748.6 2.2 fusion.111
  751.7 2.1 fusion.113
  755.2 2.2 fusion.111
  758.4 2.1 fusion.113
  761.9 2.3 fusion.111
  765.0 2.1 fusion.113
  767.9 21.2 %while.68 = (s32[]{:T(128)}, bf16[3,384,128]{1,2,0:T(8,128)(2,1)S(1)}, s32[3]{0:T(128)}, bf16[384,384]{1,0:T(8,128)(2,1)}, bf16[3584,384]{1,0:T(8,128)(2,1)S(1)}...) while((s32[]{:T(128)}, ...), condition=%wide.region_8.9_spmd, body=%wide.region_5.8_spmd.sunk | while | flops 714374400 | bytes 18965168 | solution.py:126
  770.0 1.9 fusion.116
  772.8 2.1 fusion.118
  777.0 1.9 fusion.116
  779.8 2.1 fusion.118
  784.0 1.9 fusion.116
  786.8 2.1 fusion.118
  791.2 152.8 %while.70 = (s32[]{:T(128)}, f32[3,128]{1,0:T(4,128)}, f32[3,128]{1,0:T(4,128)}, f32[3,128,128]{2,1,0:T(8,128)S(1)}, f32[64,3,128]{2,1,0:T(4,128)}, /*index=5*/f...) while((s32[]{:T(128)}, f32[3,128]{1,0:T(4,128)}, ...), condition=%wide.region_14.15_spmd, body=%wide.region_13.14_spmd.sunk | while | flops 149765 | bytes 605335 | solution.py:33
  791.2 1.3 fusion.123
  796.1 1.3 fusion.123
  798.5 1.3 fusion.123
  800.9 1.3 fusion.123
  813.0 1.3 fusion.123
  815.5 1.3 fusion.123
  822.7 1.3 fusion.123
  832.4 1.3 fusion.123
  847.0 1.3 fusion.123
  854.2 1.3 fusion.123
  859.1 1.3 fusion.123
  871.2 1.3 fusion.123
  883.3 1.3 fusion.123
  895.4 1.3 fusion.123
  897.9 1.3 fusion.123
  902.7 1.3 fusion.123
  912.4 1.3 fusion.123
  914.8 1.3 fusion.123
  919.7 1.3 fusion.123
  922.1 1.3 fusion.123
  924.6 1.3 fusion.123
  931.8 1.3 fusion.123
  (231 shorter events, 171.5 us)
Async XLA Ops:
  7.2 193.6 %all-reduce.4.cloned.1.call-start = ((), (), s32[]{:S(2)}) async-start(), calls=%async_computation | async-start | bytes 589824 | tf_op jit(solution)/shard_map/psum | solution.py:11
  8.6 781.6 %all-gather.7.cloned.1.call-start = ((), (), s32[]{:S(2)}) async-start(), calls=%async_computation.1 | async-start | bytes 12779520 | tf_op jit(solution)/shard_map/all_gather | solution.py:28
  211.6 7.8 copy-start.1
  211.6 7.8 copy-start.8
  211.6 7.8 copy-start.9
  211.7 46.0 %copy-start.12 = (s32[1,1,2,9]{3,2,1,0:T(2,128)S(1)}, s32[1,1,2,9]{3,2,1,0:T(2,128)}, u32[]{:S(2)}) copy-start(s32[1,1,2,9]{3,2,1,0:T(2,128)} %param.18) | copy-start | bytes 220
  211.7 29.4 %collective-permute-start = (bf16[2,1,1,2,384,384]{5,4,3,2,1,0:T(8,128)(2,1)}, bf16[2,1,1,2,384,384]{5,4,3,2,1,0:T(8,128)(2,1)S(1)}, u32[]{:S(2)}, u32[]{:S(2)}) collective-permute-start(bf16[2,1,1,2,384,384]{5,4,3,2,1,0:T(8,128)(2,1)} %param.16), channel_id=1, source_target_pairs={{0,64},{64,128},{128,192},{192,256},{256,320},{320,384},{384,448},... | collective-permute-start | bytes 3538952 | tf_op jit(solution)/shard_map/ppermute | solution.py:21
  213.6 39.5 %collective-permute-start.1 = (bf16[2,1,1,2,384,384]{5,4,3,2,1,0:T(8,128)(2,1)}, bf16[2,1,1,2,384,384]{5,4,3,2,1,0:T(8,128)(2,1)S(1)}, u32[]{:S(2)}, u32[]{:S(2)}) collective-permute-start(bf16[2,1,1,2,384,384]{5,4,3,2,1,0:T(8,128)(2,1)} %param.16), channel_id=1, source_target_pairs={{64,0},{128,64},{192,128},{256,192},{320,256},{384,320},{448,384},... | collective-permute-start | bytes 3538952 | tf_op jit(solution)/shard_map/ppermute | solution.py:22
  253.4 444.2 %collective-permute-start.2 = (bf16[2,3,1,2,384,384]{5,4,3,2,1,0:T(8,128)(2,1)S(1)}, bf16[2,3,1,2,384,384]{5,4,3,2,1,0:T(8,128)(2,1)}, u32[]{:S(2)}, u32[]{:S(2)}) collective-permute-start(bf16[2,3,1,2,384,384]{5,4,3,2,1,0:T(8,128)(2,1)S(1)} %constant_dynamic-update-slice_fusion.2), channel_id=1, source_target_pairs={{0,8},{8,16},{16,24},{24,32},{32,40},{40,48},{48,56},{1,9},{9,17},... | collective-permute-start | bytes 10616840 | tf_op jit(solution)/shard_map/ppermute | solution.py:21
  256.4 441.2 %collective-permute-start.3 = (bf16[2,3,1,2,384,384]{5,4,3,2,1,0:T(8,128)(2,1)S(1)}, bf16[2,3,1,2,384,384]{5,4,3,2,1,0:T(8,128)(2,1)}, u32[]{:S(2)}, u32[]{:S(2)}) collective-permute-start(bf16[2,3,1,2,384,384]{5,4,3,2,1,0:T(8,128)(2,1)S(1)} %constant_dynamic-update-slice_fusion.2), channel_id=1, source_target_pairs={{8,0},{16,8},{24,16},{32,24},{40,32},{48,40},{56,48},{9,1},{17,9},... | collective-permute-start | bytes 10616840 | tf_op jit(solution)/shard_map/ppermute | solution.py:22
  546.8 124.9 %copy-start.6 = (f32[64,3,128]{2,1,0:T(4,128)}, f32[64,3,128]{2,1,0:T(4,128)S(1)}, u32[]{:S(2)}) copy-start(f32[64,3,128]{2,1,0:T(4,128)S(1)} %all-gather.4) | copy-start | bytes 294916
  671.7 0.7 copy-start.7
  677.4 2.3 copy-start.4
  685.1 2.3 copy-start.4
  692.8 2.3 copy-start.4
  731.7 5.3 copy-start.2
  731.7 5.3 copy-start.3
  737.1 10.2 %copy-start = (f32[3584]{0:T(1024)S(1)}, f32[3584]{0:T(1024)}, u32[]{:S(2)}) copy-start(f32[3584]{0:T(1024)} %concatenate.27) | copy-start | bytes 43012
  789.1 155.0 %copy-start.10 = (f32[3,128]{1,0:T(4,128)S(1)}, f32[3,128]{1,0:T(4,128)}, u32[]{:S(2)}) copy-start(f32[3,128]{1,0:T(4,128)} %get-tuple-element.349) | copy-start | bytes 4612
  789.1 155.0 %copy-start.11 = (f32[3,128]{1,0:T(4,128)S(1)}, f32[3,128]{1,0:T(4,128)}, u32[]{:S(2)}) copy-start(f32[3,128]{1,0:T(4,128)} %get-tuple-element.352) | copy-start | bytes 4612
  789.1 155.7 %copy-start.5 = (f32[3,128,128]{1,2,0:T(8,128)S(1)}, f32[3,128,128]{1,2,0:T(8,128)}, u32[]{:S(2)}) copy-start(f32[3,128,128]{1,2,0:T(8,128)} %get-tuple-element.350) | copy-start | bytes 589828
Sparse Core Ops, SparseCore 0:
  12.0 188.6 all-reduce.3
  211.8 321.7 all-gather.6
where the time goes:
time: 958 us; the launch traced here: 952 us
  blocking collectives  404 us (42%)
  waiting for transfers between devices  223 us (23%)
  other arithmetic  183 us (19%)
  local copies, waits for them, and re-layouts  67.8 us (7%)
  matrix products  37.9 us (4%)
  between operations  14.9 us (2%)
  starting transfers between devices  12.1 us (1%)
  loops' own time  9.84 us (1%)
    all_gather x2, blocking collectives, combined_all(): gathered = jax.tree.map(lambda a: lax.all_gather(a, axis), part)  404 us
    psum x1, waiting for transfers between devices, broadcast(): return lax.psum(kept, axis)  191 us
    add x64, other arithmetic, combine(): merged_sum = sum_first * factor_first + sum_second * factor_second  80.8 us
    add x63, other arithmetic, combine(): acc_first * factor_first[..., None] + acc_second * factor_second[..., None]  71.1 us
    ppermute x2, waiting for transfers between devices, padded(): before = lax.ppermute(last, axis, up)  21.7 us
  transfers between devices with their start and end apart: 6, of which 3 were waited for; matrix products, arithmetic and copies ran while one was open for 13% of the time, Pallas kernels for 0%

commit v1 on v0

--- a/solution.py
+++ b/solution.py
@@ -8,7 +8,7 @@
 
 def broadcast(value, axis, source):
     kept = jnp.where(lax.axis_index(axis) == source, value, 0).astype(value.dtype)
-    return lax.psum(kept, axis)
+    return jnp.sum(lax.all_gather(kept, axis), axis=0)
 
 
 def padded(x, sides, width):

time: 958 us -> 896 us (0.935)
  waiting for transfers between devices: 223 us -> 407 us
  blocking collectives: 404 us -> 247 us
  other arithmetic: 183 us -> 111 us
  local copies, waits for them, and re-layouts: 67.8 us -> 54 us
    all_gather x0 -> x1, waiting for transfers between devices: none -> 213 us  [broadcast(): return jnp.sum(lax.all_gather(kept, axis), axis=0)]
    psum x1 -> x0, waiting for transfers between devices: 191 us -> none  [broadcast(): return lax.psum(kept, axis)]
    all_gather x2, blocking collectives: 404 us -> 247 us  [combined_all(): gathered = jax.tree.map(lambda a: lax.all_gather(a, axis), part)]
    ppermute x2, waiting for transfers between devices: 10.3 us -> 94.9 us  [padded(): after = lax.ppermute(initial, axis, down)]
    add x64, other arithmetic: 80.8 us -> 1.64 us  [combine(): merged_sum = sum_first * factor_first + sum_second * factor_second]
    ppermute x2, waiting for transfers between devices: 21.7 us -> 98.6 us  [padded(): before = lax.ppermute(last, axis, up)]
  transfers between devices with their start and end apart: 6 -> 6, of which waited for: 3 -> 5; matrix products, arithmetic and copies ran while one was open for 13% -> 12% of each run, Pallas kernels for 0% -> 0%
where the time goes in v1:
time: 896 us; the launch traced here: 893 us
  waiting for transfers between devices  407 us (45%)
  blocking collectives  247 us (28%)
  other arithmetic  111 us (12%)
  local copies, waits for them, and re-layouts  54 us (6%)
  matrix products  37.9 us (4%)
  between operations  14.9 us (2%)
  starting transfers between devices  12.3 us (1%)
  loops' own time  9.9 us (1%)
    all_gather x2, blocking collectives, combined_all(): gathered = jax.tree.map(lambda a: lax.all_gather(a, axis), part)  247 us
    all_gather x1, waiting for transfers between devices, broadcast(): return jnp.sum(lax.all_gather(kept, axis), axis=0)  213 us
    ppermute x2, waiting for transfers between devices, padded(): before = lax.ppermute(last, axis, up)  98.6 us
    ppermute x2, waiting for transfers between devices, padded(): after = lax.ppermute(initial, axis, down)  94.9 us
    add x63, other arithmetic, combine(): acc_first * factor_first[..., None] + acc_second * factor_second[..., None]  71.5 us
  transfers between devices with their start and end apart: 6, of which 5 were waited for; matrix products, arithmetic and copies ran while one was open for 12% of the time, Pallas kernels for 0%

profile of v1, /device:TPU:256, one launch (start us, length us, event | category | flops | bytes accessed | tf_op | source)
XLA Modules:
  0.0 892.7 jit_solution(5486430429187656467)
XLA Ops:
  8.7 1.4 fusion.88
  10.2 213.0 %all-gather.9.cloned.1.call-done = bf16[192,1,128,384]{3,2,1,0:T(8,128)(2,1)} async-done(((bf16[3,1,128,384]{3,2,1,0:T(8,128)(2,1)}), bf16[192,1,128,384]{3,2,1,0:T(8,128)(2,1)}) %all-gather.9.cloned.1.call-update) | async-done | bytes 18874384 | tf_op jit(solution)/shard_map/all_gather | solution.py:11
  223.2 7.6 bitcast_reduce_fusion
  231.6 9.1 %while.69 = (s32[]{:T(128)}, f32[3,128]{1,0:T(4,128)S(1)}, f32[3,128]{1,0:T(4,128)S(1)}, f32[3,128,128]{2,1,0:T(8,128)}, s32[3]{0:T(128)S(1)}, /*index=5*/bf16[1...) while((s32[]{:T(128)}, f32[3,128]{1,0:T(4,128)S(1)}, ...), condition=%wide.region_12.13_spmd, body=%wide.region_9.12_spmd.sunk | while | flops 176652032 | bytes 1873595 | solution.py:135
  233.1 1.2 fusion.122
  236.2 1.2 fusion.122
  239.2 1.2 fusion.122
  240.8 2.5 collective-permute-start
  243.3 5.2 collective-permute-start.1
  248.5 21.0 %collective-permute-done = bf16[2,1,1,2,384,384]{5,4,3,2,1,0:T(8,128)(2,1)S(1)} collective-permute-done((bf16[2,1,1,2,384,384]{5,4,3,2,1,0:T(8,128)(2,1)}, bf16[2,1,1,2,384,384]{5,4,3,2,1,0:T(8,128)(2,1)S(1)}, u32[]{:S(2)}, u32[]{:S(2)}) %collective-permute-start) | collective-permute-done | bytes 1179680 | tf_op jit(solution)/shard_map/ppermute | solution.py:21
  269.6 1.5 constant_dynamic-update-slice_fusion.3
  271.2 11.4 %collective-permute-done.1 = bf16[2,1,1,2,384,384]{5,4,3,2,1,0:T(8,128)(2,1)S(1)} collective-permute-done((bf16[2,1,1,2,384,384]{5,4,3,2,1,0:T(8,128)(2,1)}, bf16[2,1,1,2,384,384]{5,4,3,2,1,0:T(8,128)(2,1)S(1)}, u32[]{:S(2)}, u32[]{:S(2)}) %collective-permute-start.1) | collective-permute-done | bytes 1179680 | tf_op jit(solution)/shard_map/ppermute | solution.py:22
  282.8 3.1 collective-permute-start.2
  285.9 1.5 collective-permute-start.3
  289.3 1.3 broadcast_in_dim.78
  290.6 1.3 reshape.390
  295.2 1.9 slice_bitcast_fusion.1
  297.1 77.6 %collective-permute-done.2 = bf16[2,3,1,2,384,384]{5,4,3,2,1,0:T(8,128)(2,1)} collective-permute-done((bf16[2,3,1,2,384,384]{5,4,3,2,1,0:T(8,128)(2,1)S(1)}, bf16[2,3,1,2,384,384]{5,4,3,2,1,0:T(8,128)(2,1)}, u32[]{:S(2)}, u32[]{:S(2)}) %collective-permute-start.2) | collective-permute-done | bytes 3538976 | tf_op jit(solution)/shard_map/ppermute | solution.py:21
  374.8 83.5 %collective-permute-done.3 = bf16[2,3,1,2,384,384]{5,4,3,2,1,0:T(8,128)(2,1)} collective-permute-done((bf16[2,3,1,2,384,384]{5,4,3,2,1,0:T(8,128)(2,1)S(1)}, bf16[2,3,1,2,384,384]{5,4,3,2,1,0:T(8,128)(2,1)}, u32[]{:S(2)}, u32[]{:S(2)}) %collective-permute-start.3) | collective-permute-done | bytes 3538976 | tf_op jit(solution)/shard_map/ppermute | solution.py:22
  458.2 8.3 pad_maximum_fusion
  466.5 9.8 %fusion.87 = (bf16[1,3,3,2,384,384]{5,4,3,2,1,0:T(8,128)(2,1)}, bf16[1,3,3,2,384,384]{5,4,3,2,1,0:T(8,128)(2,1)}) fusion(bf16[2,3,3,2,384,384]{5,4,3,2,1,0:T(8,128)(2,1)} %pad_maximum_fusion), kind=kLoop, calls=%fused_computation.134 | loop fusion | bytes 21233664 | tf_op jit(solution)/shard_map/slice | solution.py:76
  476.3 5.5 gather_fusion.1
  481.7 5.3 gather_fusion.3
  487.1 5.4 gather_fusion.2
  492.5 5.4 gather_fusion
  497.9 10.3 %pad_maximum_fusion.2 = (bf16[3584,384]{1,0:T(8,128)(2,1)}, bf16[3584,384]{1,0:T(8,128)(2,1)S(1)}, bf16[3584,384]{1,0:T(8,128)(2,1)}, bf16[3584,384]{1,0:T(8,128)(2,1)}) fusion(bf16[128,384]{1,0:T(8,128)(2,1)S(1)} %copy-done.2, bf16[3456,384]{1,0:T(8,128)(2,1)} %bitcast.209, bf16[3456,384]{1,0:T(8,128)(2,1)} %bitcast.208, bf16[128,384]{1,0:T(8,128)(2,1)S(1)} %copy-done.4, ...), kind=kLoop, calls=%fused_computation.69 | loop fusion | flops 19267584 | bytes 21823488 | tf_op jit(solution)/shard_map/concatenate | solution.py:92
  508.2 20.0 %while.67 = (s32[]{:T(128)}, bf16[3,384,128]{1,2,0:T(8,128)(2,1)S(1)}, s32[3]{0:T(128)S(1)}, bf16[384,384]{1,0:T(8,128)(2,1)}, bf16[3584,384]{1,0:T(8,128)(2,1)}...) while((s32[]{:T(128)}, ...), condition=%wide.region_4.5_spmd, body=%wide.region_1.4_spmd.sunk | while | flops 714374400 | bytes 18963120 | solution.py:126
  509.5 2.3 fusion.111
  512.6 2.1 fusion.113
  516.1 2.3 fusion.111
  519.3 2.1 fusion.113
  522.8 2.3 fusion.111
  526.0 2.1 fusion.113
  529.0 19.2 %while.68 = (s32[]{:T(128)}, bf16[3,384,128]{1,2,0:T(8,128)(2,1)S(1)}, s32[3]{0:T(128)S(1)}, bf16[384,384]{1,0:T(8,128)(2,1)}, bf16[3584,384]{1,0:T(8,128)(2,1)S...) while((s32[]{:T(128)}, ...), condition=%wide.region_8.9_spmd, body=%wide.region_5.8_spmd.sunk | while | flops 714374400 | bytes 18965168 | solution.py:126
  530.5 1.9 fusion.116
  533.3 2.1 fusion.118
  536.8 1.9 fusion.116
  539.6 2.1 fusion.118
  543.2 1.9 fusion.116
  546.0 2.1 fusion.118
  550.4 122.2 %all-gather.5 = f32[64,3,128]{2,1,0:T(4,128)S(1)} all-gather(f32[1,3,128]{2,1,0:T(4,128)S(1)} %bitcast.220), channel_id=4, replica_groups=mesh['tm'=8,'height'=8,'head'=8] {'tm','height'}, dimensions={0}, use_global_device_ids=true | all-gather | bytes 99840 | tf_op jit(solution)/shard_map/all_gather | solution.py:28
  672.6 124.4 %all-gather.4 = f32[64,3,128]{2,1,0:T(4,128)S(1)} all-gather(f32[1,3,128]{2,1,0:T(4,128)S(1)} %bitcast.219), channel_id=3, replica_groups=mesh['tm'=8,'height'=8,'head'=8] {'tm','height'}, dimensions={0}, use_global_device_ids=true | all-gather | bytes 99840 | tf_op jit(solution)/shard_map/all_gather | solution.py:28
  797.0 12.2 %while.71 = (s32[]{:T(128)}, f32[3,128]{1,0:T(4,128)S(1)}, f32[3,128]{1,0:T(4,128)S(1)}, f32[3,128,128]{1,2,0:T(8,128)}, s32[3]{0:T(128)S(1)}, /*index=5*/bf16[1...) while((s32[]{:T(128)}, f32[3,128]{1,0:T(4,128)S(1)}, ...), condition=%wide.region_18.19_spmd, body=%wide.region_15.18_spmd.sunk | while | flops 29441796 | bytes 399035 | solution.py:144
  799.2 1.8 fusion.128
  803.3 1.8 fusion.128
  807.3 1.8 fusion.128
  810.2 74.7 %while.70 = (s32[]{:T(128)}, f32[3,128]{1,0:T(4,128)S(1)}, f32[3,128]{1,0:T(4,128)S(1)}, f32[3,128,128]{2,1,0:T(8,128)S(1)}, f32[64,3,128]{2,1,0:T(4,128)S(1)}, ...) while((s32[]{:T(128)}, f32[3,128]{1,0:T(4,128)S(1)}, ...), condition=%wide.region_14.15_spmd, body=%wide.region_13.14_spmd.sunk | while | flops 149765 | bytes 605335 | solution.py:33
  810.3 1.1 fusion.124
  811.5 1.1 fusion.124
  812.6 1.1 fusion.124
  815.0 1.1 fusion.124
  816.2 1.1 fusion.124
  817.4 1.1 fusion.124
  818.6 1.1 fusion.124
  819.8 1.1 fusion.124
  822.1 1.1 fusion.124
  823.3 1.1 fusion.124
  824.5 1.1 fusion.124
  825.7 1.1 fusion.124
  826.9 1.1 fusion.124
  829.2 1.1 fusion.124
  830.4 1.1 fusion.124
  831.6 1.1 fusion.124
  832.8 1.1 fusion.124
  (224 shorter events, 84.2 us)
Async XLA Ops:
  7.2 216.0 %all-gather.9.cloned.1.call-start = ((), (), s32[]{:S(2)}) async-start(), calls=%async_computation | async-start | bytes 19169280 | tf_op jit(solution)/shard_map/all_gather | solution.py:11
  8.6 800.6 %all-gather.11.cloned.1.call-start = ((), (), s32[]{:S(2)}) async-start(), calls=%async_computation.1 | async-start | bytes 12779520 | tf_op jit(solution)/shard_map/all_gather | solution.py:28
  240.7 7.8 copy-start.1
  240.7 7.8 copy-start.6
  240.7 7.8 copy-start.8
  240.8 46.6 %copy-start.10 = (s32[1,1,2,9]{3,2,1,0:T(2,128)S(1)}, s32[1,1,2,9]{3,2,1,0:T(2,128)}, u32[]{:S(2)}) copy-start(s32[1,1,2,9]{3,2,1,0:T(2,128)} %param.18) | copy-start | bytes 220
  240.8 28.7 %collective-permute-start = (bf16[2,1,1,2,384,384]{5,4,3,2,1,0:T(8,128)(2,1)}, bf16[2,1,1,2,384,384]{5,4,3,2,1,0:T(8,128)(2,1)S(1)}, u32[]{:S(2)}, u32[]{:S(2)}) collective-permute-start(bf16[2,1,1,2,384,384]{5,4,3,2,1,0:T(8,128)(2,1)} %param.16), channel_id=1, source_target_pairs={{0,64},{64,128},{128,192},{192,256},{256,320},{320,384},{384,448},... | collective-permute-start | bytes 3538952 | tf_op jit(solution)/shard_map/ppermute | solution.py:21
  243.3 39.3 %collective-permute-start.1 = (bf16[2,1,1,2,384,384]{5,4,3,2,1,0:T(8,128)(2,1)}, bf16[2,1,1,2,384,384]{5,4,3,2,1,0:T(8,128)(2,1)S(1)}, u32[]{:S(2)}, u32[]{:S(2)}) collective-permute-start(bf16[2,1,1,2,384,384]{5,4,3,2,1,0:T(8,128)(2,1)} %param.16), channel_id=1, source_target_pairs={{64,0},{128,64},{192,128},{256,192},{320,256},{384,320},{448,384},... | collective-permute-start | bytes 3538952 | tf_op jit(solution)/shard_map/ppermute | solution.py:22
  282.8 92.0 %collective-permute-start.2 = (bf16[2,3,1,2,384,384]{5,4,3,2,1,0:T(8,128)(2,1)S(1)}, bf16[2,3,1,2,384,384]{5,4,3,2,1,0:T(8,128)(2,1)}, u32[]{:S(2)}, u32[]{:S(2)}) collective-permute-start(bf16[2,3,1,2,384,384]{5,4,3,2,1,0:T(8,128)(2,1)S(1)} %constant_dynamic-update-slice_fusion.2), channel_id=1, source_target_pairs={{0,8},{8,16},{16,24},{24,32},{32,40},{40,48},{48,56},{1,9},{9,17},... | collective-permute-start | bytes 10616840 | tf_op jit(solution)/shard_map/ppermute | solution.py:21
  285.9 172.4 %collective-permute-start.3 = (bf16[2,3,1,2,384,384]{5,4,3,2,1,0:T(8,128)(2,1)S(1)}, bf16[2,3,1,2,384,384]{5,4,3,2,1,0:T(8,128)(2,1)}, u32[]{:S(2)}, u32[]{:S(2)}) collective-permute-start(bf16[2,3,1,2,384,384]{5,4,3,2,1,0:T(8,128)(2,1)S(1)} %constant_dynamic-update-slice_fusion.2), channel_id=1, source_target_pairs={{8,0},{16,8},{24,16},{32,24},{40,32},{48,40},{56,48},{9,1},{17,9},... | collective-permute-start | bytes 10616840 | tf_op jit(solution)/shard_map/ppermute | solution.py:22
  492.5 5.4 copy-start.2
  492.5 5.4 copy-start.4
  497.9 10.3 %copy-start = (f32[3584]{0:T(1024)S(1)}, f32[3584]{0:T(1024)}, u32[]{:S(2)}) copy-start(f32[3584]{0:T(1024)} %concatenate.27) | copy-start | bytes 43012
  528.2 0.7 copy-start.3
  529.0 21.4 %copy-start.9 = (f32[3,128]{1,0:T(4,128)S(1)}, f32[3,128]{1,0:T(4,128)}, u32[]{:S(2)}) copy-start(f32[3,128]{1,0:T(4,128)} %copy-done.8) | copy-start | bytes 4612
  529.0 143.6 %copy-start.7 = (f32[3,128]{1,0:T(4,128)S(1)}, f32[3,128]{1,0:T(4,128)}, u32[]{:S(2)}) copy-start(f32[3,128]{1,0:T(4,128)} %copy-done.6) | copy-start | bytes 4612
  809.2 75.9 %copy-start.5 = (f32[3,128,128]{1,2,0:T(8,128)S(1)}, f32[3,128,128]{1,2,0:T(8,128)}, u32[]{:S(2)}) copy-start(f32[3,128,128]{1,2,0:T(8,128)} %get-tuple-element.350) | copy-start | bytes 589828
Sparse Core Ops, SparseCore 0:
  10.7 212.4 all-gather.8
  240.9 317.7 all-gather.10
